TPU v7x, 1024 devices: a whole 4x4x32 slice. The times are simulated.
1024 devices in a mesh: scen: 32 (over z_lo, x), row: 32 (over y, z_hi, core).
Axes of the slice: x: 4, y: 4, z: 32 (z_hi: 4, z_lo: 8; z = z_hi * 8 + z_lo), core: 2. Of those that a mesh axis runs over, the one named last changes fastest.
Arguments:
- border: bfloat16 [512, 8192, 128], P('scen', 'row'), may hold values from -0.119628906 to 0.119628906
- col_index: int32 [512, 128], P('scen'), may hold values from 0 to 4095
- barrier: float32 [4096], replicated, may hold values from 0.3 to 3
- counts: int32 [32], replicated, may hold values from 1 to 16, as said below
- inverse: bfloat16 [1024, 1024], replicated, may hold values from -0.140625 to 0.140625
- slab: float32 [8192, 4096], P('row', 'scen'), may hold values from -1.5 to 1.5
Outputs:
- updated: float32 [8192, 4096], P('row', 'scen')
Inputs may be any that keep to these rules, and one draw needn't show every extreme that they name: `counts`: the scenario groups whose index differs by a multiple of 4 from one drawn index hold 16 live blocks; every other group holds 1 to 4.
All inputs are finite; a program needn't handle non-finite values.
Results may differ from a plain program's by a relative error of at most 0.0064.
Values may be sent and summed in bfloat16 or wider, within the bound.
A program may use at most 32 MiB of HBM per device.

v0:
```python
import jax
import jax.numpy as jnp
from jax import lax
from jax.sharding import PartitionSpec as P

blocks_per_product = 4


def passed_along(block, axis, distance):
    devices = range(lax.axis_size(axis))
    route = [((i - distance) % len(devices), i) for i in devices]
    return lax.ppermute(block, axis, route)


def broadcast(array, axis, root):
    return lax.dynamic_index_in_dim(lax.all_gather(array, axis), root, 0, keepdims=False)


def move_parcel(parcel, offset):
    return passed_along(parcel, "scen", offset)


def body(border, col_index, barrier, counts, inverse, slab):
    scen_count = lax.axis_size("scen")
    row_count = lax.axis_size("row")
    my_scen = lax.axis_index("scen")
    slot_count, local_rows, block_width = border.shape
    panel_width = inverse.shape[0]
    share_width = panel_width // row_count
    weights = barrier[col_index]
    scaled = (border.astype(jnp.float32) * weights[:, None, :]).astype(jnp.bfloat16)
    slot_ids = jnp.arange(slot_count, dtype=jnp.int32)
    own_count = counts[my_scen]
    light_most = slot_count // 4
    carry_most = (3 * slot_count + 15) // 16
    keep_most = light_most + carry_most
    carry_ids = jnp.arange(carry_most, dtype=jnp.int32)
    candidates = [scaled[:keep_most]]
    live_masks = [slot_ids[:keep_most] < own_count]
    for offset in (1, 2, 3):
        first_slot = keep_most + (offset - 1) * carry_most
        parcel = scaled[first_slot : first_slot + carry_most]
        candidates.append(move_parcel(parcel, offset))
        source_count = counts[(my_scen - offset) % scen_count]
        live_masks.append(first_slot + carry_ids < source_count)
    present = jnp.concatenate(live_masks)
    placing = jnp.argsort(jnp.where(present, 0, 1).astype(jnp.int32), stable=True)[:keep_most]
    held = jnp.take(jnp.concatenate(candidates, axis=0), placing, axis=0)
    held_count = jnp.sum(present.astype(jnp.int32))
    held_slots = held.shape[0]
    held_ids = jnp.arange(held_slots, dtype=jnp.int32)
    held = jnp.where((held_ids < held_count)[:, None, None], held, jnp.zeros_like(held))
    heads = held[:, :share_width, :]
    padded_slots = (held_slots + blocks_per_product - 1) // blocks_per_product * blocks_per_product
    held_padded = jnp.pad(held, ((0, padded_slots - held_slots), (0, 0), (0, 0)))
    group_total = (held_count + blocks_per_product - 1) // blocks_per_product
    piece = lax.all_gather(heads, "row", axis=1, tiled=True)
    piece_width = piece.shape[1]
    piece_padded = jnp.pad(piece, ((0, padded_slots - piece.shape[0]), (0, 0), (0, 0)))

    def one_group(number, running):
        left_part = lax.dynamic_slice_in_dim(
            held_padded, number * blocks_per_product, blocks_per_product, 0
        )
        right_part = lax.dynamic_slice_in_dim(
            piece_padded, number * blocks_per_product, blocks_per_product, 0
        )
        return running + jnp.einsum(
            "kib,kjb->ij", left_part, right_part, preferred_element_type=jnp.float32
        )

    block_sum = lax.fori_loop(
        0, group_total, one_group, jnp.zeros((local_rows, piece_width), jnp.float32)
    )
    summed = lax.psum(block_sum, "scen")
    rounded = summed.astype(jnp.bfloat16)
    finished = jnp.dot(rounded, inverse, preferred_element_type=jnp.float32).astype(jnp.bfloat16)
    trail_width = slab.shape[1]
    first_row = my_scen * trail_width
    source_row = first_row // local_rows
    wanted = lax.dynamic_slice_in_dim(rounded, first_row % local_rows, trail_width, 0)
    trailing = broadcast(wanted, "row", source_row)
    update = jnp.einsum("ip,jp->ij", finished, trailing, preferred_element_type=jnp.float32)
    return slab - update


def solution(mesh):
    return jax.shard_map(
        body,
        mesh=mesh,
        in_specs=(P("scen", "row", None), P("scen", None), P(), P(), P(), P("row", "scen")),
        out_specs=P("row", "scen"),
        check_vma=False,
    )
```

profile of v0, /device:TPU:33, one launch (start us, length us, event | category | flops | bytes accessed | tf_op | source)
XLA Modules:
  0.0 683.7 jit_solution(17483694207736450970)
XLA Ops:
  6.5 0.0 copy-start
  6.5 0.0 copy-start.1
  6.5 0.0 all-gather.4.cloned.1.call-start
  6.5 0.9 fusion.9
  7.4 0.0 copy-done.1
  7.4 11.8 %gather_fusion = f32[2048]{0:T(1024)S(1)} fusion(f32[4096]{0:T(1024)S(1)} %copy-done.1, s32[2048]{0:T(1024)S(1)} %fusion.9), kind=kCustom, calls=%fused_computation | custom fusion | bytes 24576 | tf_op jit(solution)/shard_map/gather | solution.py:30
  19.2 0.0 copy-start.2
  19.2 1.5 multiply_convert_fusion
  20.7 0.8 fusion.11
  21.5 3.1 collective-permute-start
  24.6 4.7 collective-permute-start.2
  29.4 3.4 collective-permute-start.1
  32.9 0.8 slice.32
  33.7 0.0 copy-done.2
  33.7 0.7 fusion.12
  34.3 0.7 add_compare_fusion.2
  35.0 0.7 slice_compare_fusion
  35.7 1.2 add_compare_fusion
  36.9 0.1 broadcast_select_fusion
  37.0 0.7 convert_reduce_fusion
  37.7 1.2 sort.17
  38.9 0.7 iota_compare_fusion
  39.6 0.0 collective-permute-done
  39.6 0.0 collective-permute-done.2
  39.7 0.0 collective-permute-done.1
  39.7 1.4 pad_maximum_fusion
  41.0 1.4 gather_fusion.1
  42.4 1.1 select_select_fusion
  43.6 0.6 slice.36
  44.2 0.0 all-gather.4.cloned.1.call-update
  44.2 0.0 all-gather.6.cloned.1.call-start
  45.0 0.8 pad.8
  45.8 139.0 %all-gather.4.cloned.1.call-done = bf16[7,1024,128]{2,1,0:T(8,128)(2,1)} async-done(((bf16[7,32,128]{2,1,0:T(8,128)(2,1)}), bf16[7,1024,128]{2,1,0:T(8,128)(2,1)}) %all-gather.4.cloned.1.call-update) | async-done | bytes 1835024 | tf_op jit(solution)/shard_map/all_gather | solution.py:57
  184.8 3.0 pad.9
  187.7 0.1 broadcast_in_dim.39
  187.9 3.8 while.10
  187.9 1.9 fusion.20
  189.8 1.9 fusion.20
  191.7 0.0 copy-start.3
  191.7 199.4 %all-reduce.3 = bf16[256,1024]{1,0:T(8,128)(2,1)} all-reduce(f32[256,1024]{1,0:T(8,128)S(1)} %get-tuple-element.35), channel_id=1, replica_groups=mesh['scen'=32,'row'=32] {'scen'}, use_global_device_ids=true, to_apply=%region_4.5 | all-reduce | flops 262144 | bytes 1572864 | tf_op jit(solution)/shard_map/psum | solution.py:75
  391.1 1.7 constant_dynamic-slice_fusion
  392.8 0.0 all-gather.6.cloned.1.call-update
  392.8 281.3 %all-gather.6.cloned.1.call-done = bf16[4096,1024]{1,0:T(8,128)(2,1)} async-done(((bf16[128,1024]{1,0:T(8,128)(2,1)}), bf16[4096,1024]{1,0:T(8,128)(2,1)}) %all-gather.6.cloned.1.call-update) | async-done | bytes 8388624 | tf_op jit(solution)/shard_map/all_gather | solution.py:16
  674.2 0.0 copy-done
  674.2 0.0 copy-done.3
  674.2 2.7 fusion.5
  (4 shorter events, 0.0 us)
Async XLA Ops:
  6.5 667.6 %copy-start = (bf16[1024,1024]{1,0:T(8,128)(2,1)S(1)}, bf16[1024,1024]{1,0:T(8,128)(2,1)}, u32[]{:S(2)}) copy-start(bf16[1024,1024]{1,0:T(8,128)(2,1)} %param.12) | copy-start | bytes 6291460
  6.5 0.9 copy-start.1
  6.5 178.2 %all-gather.4.cloned.1.call-start = ((), (), s32[]{:S(2)}) async-start(), calls=%async_computation | async-start | bytes 1892352 | tf_op jit(solution)/shard_map/all_gather | solution.py:57
  19.2 14.5 %copy-start.2 = (s32[32]{0:T(128)S(1)}, s32[32]{0:T(128)}, u32[]{:S(2)}) copy-start(s32[32]{0:T(128)} %param.11) | copy-start | bytes 388
  21.5 18.1 %collective-permute-start = (bf16[3,256,128]{2,1,0:T(8,128)(2,1)}, bf16[3,256,128]{2,1,0:T(8,128)(2,1)S(1)}, u32[]{:S(2)}, u32[]{:S(2)}) collective-permute-start(bf16[3,256,128]{2,1,0:T(8,128)(2,1)} %get-tuple-element.50), channel_id=1, source_target_pairs={{992,0},{0,32},{32,64},{64,96},{96,128},{128,160},{160,192},{192,2... | collective-permute-start | bytes 589832 | tf_op jit(solution)/shard_map/ppermute | solution.py:12
  24.6 15.0 %collective-permute-start.2 = (bf16[3,256,128]{2,1,0:T(8,128)(2,1)}, bf16[3,256,128]{2,1,0:T(8,128)(2,1)}, u32[]{:S(2)}, u32[]{:S(2)}) collective-permute-start(bf16[3,256,128]{2,1,0:T(8,128)(2,1)} %get-tuple-element.51), channel_id=1, source_target_pairs={{928,0},{960,32},{992,64},{0,96},{32,128},{64,160},{96,192},{128,2... | collective-permute-start | bytes 589832 | tf_op jit(solution)/shard_map/ppermute | solution.py:12
  29.4 10.3 %collective-permute-start.1 = (bf16[3,256,128]{2,1,0:T(8,128)(2,1)S(1)}, bf16[3,256,128]{2,1,0:T(8,128)(2,1)}, u32[]{:S(2)}, u32[]{:S(2)}) collective-permute-start(bf16[3,256,128]{2,1,0:T(8,128)(2,1)S(1)} %get-tuple-element.52), channel_id=1, source_target_pairs={{960,0},{992,32},{0,64},{32,96},{64,128},{96,160},{128,192},{160,2... | collective-permute-start | bytes 589832 | tf_op jit(solution)/shard_map/ppermute | solution.py:12
  44.2 629.9 %all-gather.6.cloned.1.call-start = ((), (), s32[]{:S(2)}) async-start(), calls=%async_computation.1 | async-start | bytes 8650752 | tf_op jit(solution)/shard_map/all_gather | solution.py:16
  191.7 482.5 %copy-start.3 = (f32[256,128]{1,0:T(8,128)S(1)}, f32[256,128]{1,0:T(8,128)}, u32[]{:S(2)}) copy-start(f32[256,128]{1,0:T(8,128)} %param.13) | copy-start | bytes 393220
Sparse Core Ops, SparseCore 0:
  44.3 140.3 all-gather.3
  392.9 281.1 all-gather.5
where the time goes:
time: 684 us
  waiting for transfers between devices  420 us (61%)
  blocking collectives  199 us (29%)
  local copies, waits for them, and re-layouts  21.6 us (3%)
  between operations  14.4 us (2%)
  starting transfers between devices  11.3 us (2%)
  other arithmetic  10.2 us (1%)
    all_gather x1, waiting for transfers between devices, broadcast(): lax.all_gather(array, axis)  281 us
    psum x1, blocking collectives, body(): summed = lax.psum(block_sum, 'scen')  199 us
    all_gather x1, waiting for transfers between devices, body(): piece = lax.all_gather(heads, 'row', axis=1, tiled=True)  139 us
  transfers between devices with their start and end apart: 5, of which 2 were waited for; matrix products, arithmetic and copies ran while one was open for 1% of the time, Pallas kernels for 0%

commit v1 on v0

v1 whole, which is shorter than its diff:
```python
import jax
import jax.numpy as jnp
from jax import lax
from jax.experimental import pallas as pl
from jax.experimental.pallas import tpu as pltpu
from jax.sharding import PartitionSpec as P

X, ZL, Y, ZH, CORES = 4, 8, 4, 4, 2
OWN, EXTRA, SURPLUS = 4, 3, 3
BW = 128
W0, W1 = OWN * BW, EXTRA * BW
ROWS, SHARE, PANEL = 256, 32, 1024
SEG = PANEL // ZH
BLK, PIECE = 64, 16
OWNERS, FIRST_OWNER = 4, 2
F32, BF16 = jnp.float32, jnp.bfloat16


def nt_dot(a, b):
    return lax.dot_general(a, b, (((1,), (1,)), ((), ())), preferred_element_type=F32)


def kernel(
    counts, index, table, border, inverse, slab, out,
    kept, parcels, arrived, h0, h1, part, xin, xsum, zin, own, zg, full, trail, inv, acc,
    send_sems, inv_sem, head_sem, body_sem, z_sems, y_sems, c_sems,
    xr_sems, zr_sems, zg_sems, xg_sems, tz_sems, tc_sems,
):
    sc, rw = lax.axis_index("scen"), lax.axis_index("row")
    x, zl = sc % X, sc // X
    y, zh, c = rw // (ZH * CORES), (rw // CORES) % ZH, rw % CORES

    def dev(x_=x, zl_=zl, y_=y, zh_=zh, c_=c):
        return (zl_ * X + x_, (y_ * ZH + zh_) * CORES + c_)

    def xp(d):
        return (x + d) % X

    def yp(d):
        return (y + d) % Y

    def zp(d):
        return (zh + d + ZH) % ZH

    pending = []

    def send(src, dst, sem, target, pred=None):
        copy = pltpu.make_async_remote_copy(
            src_ref=src, dst_ref=dst, send_sem=send_sems.at[len(pending)], recv_sem=sem,
            device_id=target, device_id_type=pl.DeviceIdType.MESH,
        )
        pending.append((pred, copy))
        if pred is None:
            copy.start()
        else:
            pl.when(pred)(copy.start)

    def keep(src, dst, sem, pred):
        copy = pltpu.make_async_copy(src, dst, sem)
        pl.when(pred)(copy.start)

    def arrive(ref, sem):
        pltpu.make_async_copy(ref, ref, sem).wait()

    barrier = pltpu.get_barrier_semaphore()
    peers = [dev(x_=xp(d), c_=cc) for d in range(1, X) for cc in range(CORES)]
    peers += [dev(c_=1 - c)]
    peers += [dev(zl_=(zl + d) % ZL) for d in range(1, ZL)]
    peers += [dev(zh_=zp(1)), dev(zh_=zp(-1))]
    peers += [dev(y_=yp(d)) for d in range(1, Y)]
    for peer in peers:
        pl.semaphore_signal(barrier, inc=1, device_id=peer, device_id_type=pl.DeviceIdType.MESH)

    inv_copies = [
        pltpu.make_async_copy(inverse.at[:, b], inv.at[b], inv_sem.at[b]) for b in range(ZH)
    ]
    for copy in inv_copies:
        copy.start()

    indices = index[...]
    high, low = indices // BW, indices % BW
    weights = jnp.zeros(indices.shape, F32)
    for h in range(table.shape[0]):
        row = jnp.broadcast_to(table[h : h + 1, :], indices.shape)
        picked = jnp.take_along_axis(row, low, axis=1, mode="promise_in_bounds")
        weights = jnp.where(high == h, picked, weights)
    slots = lax.broadcasted_iota(jnp.int32, indices.shape, 0)
    weights = jnp.where(slots < counts[sc], weights, 0.0)

    def scaled(k, first, last):
        rows = border[k, first:last, :].astype(F32)
        return (rows * weights[k : k + 1, :]).astype(BF16)

    def lanes(k):
        return slice(k * BW, (k + 1) * BW)

    for k in range(OWN):
        h0[zh, y, c, :, lanes(k)] = scaled(k, 0, SHARE)
    for o in range(SURPLUS):
        for e in range(EXTRA):
            parcels[o, 0:SHARE, lanes(e)] = scaled(OWN + EXTRA * (o + 1) + e, 0, SHARE)
    pl.semaphore_wait(barrier, len(peers))

    heads = ((h0, 0), (h1, 1))
    halves = ((0, PIECE), (PIECE, SHARE))

    def z_start(h, k):
        for a, step in ((0, 1), (1, -1), (1, 1), (0, -1)):
            lo, hi = halves[a]
            ref = h.at[zh, y, c, lo:hi]
            send(ref, ref, z_sems.at[k, a, 0 if step == 1 else 1], dev(zh_=zp(step)))

    def z_relay(h, k):
        for a, step in ((0, 1), (1, -1)):
            lo, hi = halves[a]
            ref = h.at[zp(-step), y, c, lo:hi]
            arrive(ref, z_sems.at[k, a, 0 if step == 1 else 1])
            send(ref, ref, z_sems.at[k, a, 2], dev(zh_=zp(step)))

    def z_rest(h, k, origin):
        if origin == 2:
            for a in range(2):
                lo, hi = halves[a]
                arrive(h.at[zp(2), y, c, lo:hi], z_sems.at[k, a, 2])
        else:
            a, way = (1, 0) if origin == -1 else (0, 1)
            lo, hi = halves[a]
            arrive(h.at[zp(origin), y, c, lo:hi], z_sems.at[k, a, way])

    origins = (0, -1, 1, 2)

    def y_start(h, k, n):
        ref = h.at[zp(origins[n]), y, c]
        for d in (1, 3, 2):
            send(ref, ref, y_sems.at[k, n], dev(y_=yp(d)))

    def c_start(h, k, n):
        z = zp(origins[n])
        arrive(h.at[z, 0 : Y - 1, 0], y_sems.at[k, n])
        ref = h.at[z, :, c]
        send(ref, ref, c_sems.at[k, n], dev(c_=1 - c))

    z_start(h0, 0)
    for o in range(SURPLUS):
        send(parcels.at[o, 0:SHARE], arrived.at[o, 0:SHARE], head_sem, dev(x_=xp(o + 1)))
    y_start(h0, 0, 0)
    for o in range(SURPLUS):
        for e in range(EXTRA):
            parcels[o, SHARE:ROWS, lanes(e)] = scaled(OWN + EXTRA * (o + 1) + e, SHARE, ROWS)
        send(parcels.at[o, SHARE:ROWS], arrived.at[o, SHARE:ROWS], body_sem, dev(x_=xp(o + 1)))

    def with_parcels(first, last):
        mine = [scaled(OWN + e, first, last) for e in range(EXTRA)]
        total = jnp.concatenate(mine, axis=1)
        for o in range(SURPLUS):
            total = total + arrived[o, first:last, :]
        return total

    arrive(arrived.at[:, 0:SHARE], head_sem)
    extra_heads = with_parcels(0, SHARE)
    h1[zh, y, c] = extra_heads
    kept[0:SHARE, W0 : W0 + W1] = extra_heads
    z_start(h1, 1)
    y_start(h1, 1, 0)
    for k in range(OWN):
        kept[:, lanes(k)] = scaled(k, 0, ROWS)
    arrive(arrived.at[:, SHARE:ROWS], body_sem)
    kept[SHARE:ROWS, W0 : W0 + W1] = with_parcels(SHARE, ROWS)
    c_start(h0, 0, 0)
    c_start(h1, 1, 0)

    left = x // CORES
    upper = x % CORES

    def product(n):
        z = zp(origins[n])
        for h, k in heads:
            arrive(h.at[z, :, 1 - c], c_sems.at[k, n])
        a = h0[z].reshape(SEG, W0)
        b = h1[z].reshape(SEG, W1)
        block = nt_dot(kept[:, 0:W0], a) + nt_dot(kept[:, W0 : W0 + W1], b)
        part[n] = block.astype(BF16).reshape(4, BLK, SEG)
        for b in range(4):
            half, g = b // 2, b % 2
            tx = 2 * c + half
            here = jnp.logical_and(tx == x, g == c)
            dst = xin.at[n, x]
            send(part.at[n, b], dst, xr_sems.at[n], dev(x_=tx, c_=g), jnp.logical_not(here))
            keep(part.at[n, b], dst, xr_sems.at[n], here)

    def x_reduce(n):
        arrive(xin.at[n], xr_sems.at[n])
        total = xin[n, 0].astype(F32)
        for s in range(1, X):
            total = total + xin[n, s].astype(F32)
        xsum[n] = total.astype(BF16).reshape(OWNERS, PIECE, SEG)
        for j in range(OWNERS):
            here = zl == FIRST_OWNER + j
            dst = zin.at[n, zl]
            target = dev(zl_=FIRST_OWNER + j)
            send(xsum.at[n, j], dst, zr_sems.at[n], target, jnp.logical_not(here))
            keep(xsum.at[n, j], dst, zr_sems.at[n], here)

    owner = jnp.logical_and(zl >= FIRST_OWNER, zl < FIRST_OWNER + OWNERS)
    seat = jnp.clip(zl - FIRST_OWNER, 0, OWNERS - 1)

    def z_reduce(n):
        @pl.when(owner)
        def _():
            arrive(zin.at[n], zr_sems.at[n])
            total = zin[n, 0].astype(F32)
            for s in range(1, ZL):
                total = total + zin[n, s].astype(F32)
            own[n] = total.astype(BF16)

        dst = zg.at[n, seat]
        for d in range(1, ZL):
            send(own.at[n], dst, zg_sems.at[n], dev(zl_=(zl + d) % ZL), owner)
        keep(own.at[n], dst, zg_sems.at[n], owner)

    def x_gather(n):
        arrive(zg.at[n], zg_sems.at[n])
        dst = full.at[n, 2 * upper + c]
        for d in range(1, X):
            send(zg.at[n], dst, xg_sems.at[n], dev(x_=xp(d), c_=left))
        send(zg.at[n], dst, xg_sems.at[n], dev(c_=1 - c), left != c)
        keep(zg.at[n], dst, xg_sems.at[n], left == c)

    on_line = y == zl // ZH
    lag = (zh - zl % ZH + ZH) % ZH

    def t_segment(n):
        return (zl % ZH + origins[n] + ZH) % ZH

    def t_source(n):
        source = jnp.logical_and(on_line, lag == 0)
        dst = trail.at[t_segment(n), c]
        send(zg.at[n], dst, tz_sems.at[n], dev(zh_=zp(1)), source)
        send(zg.at[n], dst, tz_sems.at[n], dev(zh_=zp(-1)), source)
        keep(zg.at[n], dst, tz_sems.at[n], source)

    def t_spread(n):
        ref = trail.at[t_segment(n), c]
        arrive(ref, tz_sems.at[n])
        for a, step, at in ((0, 1, 1), (1, -1, 3)):
            cut = trail.at[t_segment(n), c, 2 * a : 2 * a + 2]
            pred = jnp.logical_and(on_line, lag == at)
            send(cut, cut, tz_sems.at[n], dev(zh_=zp(step)), pred)
        for d in (1, 3, 2):
            send(ref, ref, tz_sems.at[n], dev(y_=yp(d)), on_line)
        send(ref, ref, tc_sems.at[n], dev(c_=1 - c))

    def finish_part(n):
        if n == 0:
            for copy in inv_copies:
                copy.wait()
        arrive(full.at[n], xg_sems.at[n])
        step = jnp.dot(
            full[n].reshape(ROWS, SEG), inv[zp(origins[n])].reshape(SEG, PANEL),
            preferred_element_type=F32,
        )
        if n == 0:
            acc[...] = step
        else:
            acc[...] += step

    product(0)
    z_relay(h0, 0)
    z_rest(h0, 0, -1)
    y_start(h0, 0, 1)
    z_rest(h0, 0, 1)
    y_start(h0, 0, 2)
    x_reduce(0)
    z_relay(h1, 1)
    z_rest(h1, 1, -1)
    y_start(h1, 1, 1)
    z_rest(h1, 1, 1)
    y_start(h1, 1, 2)
    c_start(h0, 0, 1)
    c_start(h0, 0, 2)
    c_start(h1, 1, 1)
    c_start(h1, 1, 2)
    product(1)
    product(2)
    z_reduce(0)
    z_rest(h0, 0, 2)
    y_start(h0, 0, 3)
    z_rest(h1, 1, 2)
    y_start(h1, 1, 3)
    x_reduce(1)
    x_reduce(2)
    c_start(h0, 0, 3)
    c_start(h1, 1, 3)
    product(3)
    x_gather(0)
    t_source(0)
    z_reduce(1)
    z_reduce(2)
    x_reduce(3)
    for n in (1, 2):
        x_gather(n)
        t_source(n)
    z_reduce(3)
    for n in range(3):
        finish_part(n)
    x_gather(3)
    t_source(3)
    t_spread(0)
    t_spread(1)
    t_spread(2)
    finish_part(3)
    finished = acc[...].astype(BF16)
    t_spread(3)
    for n in range(4):
        arrive(trail.at[t_segment(n), 1 - c], tc_sems.at[n])
    segments = [trail[b].reshape(2 * BLK, SEG).astype(F32) for b in range(ZH)]
    update = jnp.zeros(out.shape, F32)
    for yy in range(Y):
        for pair in range(ZH // 2):
            cut = slice(yy * BLK, (yy + 1) * BLK)
            columns = jnp.concatenate([segments[2 * pair][:, cut], segments[2 * pair + 1][:, cut]], axis=1)
            at = (yy * (ZH // 2) + pair) * BW
            update = update + nt_dot(finished[:, at : at + BW], columns.astype(BF16))
    out[...] = slab[...] - update

    for pred, copy in pending:
        if pred is None:
            copy.wait_send()
        else:
            pl.when(pred)(copy.wait_send)


def body(border, col_index, barrier, counts, inverse, slab):
    vmem = pl.BlockSpec(memory_space=pltpu.VMEM)
    dma = pltpu.SemaphoreType.DMA
    return pl.pallas_call(
        kernel,
        out_shape=jax.ShapeDtypeStruct(slab.shape, slab.dtype),
        in_specs=[
            pl.BlockSpec(memory_space=pltpu.SMEM), vmem, vmem, vmem,
            pl.BlockSpec(memory_space=pl.ANY), vmem,
        ],
        out_specs=vmem,
        scratch_shapes=[
            pltpu.VMEM((ROWS, W0 + W1), BF16),
            pltpu.VMEM((SURPLUS, ROWS, W1), BF16),
            pltpu.VMEM((SURPLUS, ROWS, W1), BF16),
            pltpu.VMEM((ZH, Y, CORES, SHARE, W0), BF16),
            pltpu.VMEM((ZH, Y, CORES, SHARE, W1), BF16),
            pltpu.VMEM((ZH, 4, BLK, SEG), BF16),
            pltpu.VMEM((ZH, X, BLK, SEG), BF16),
            pltpu.VMEM((ZH, OWNERS, PIECE, SEG), BF16),
            pltpu.VMEM((ZH, ZL, PIECE, SEG), BF16),
            pltpu.VMEM((ZH, PIECE, SEG), BF16),
            pltpu.VMEM((ZH, OWNERS, PIECE, SEG), BF16),
            pltpu.VMEM((ZH, 4, OWNERS, PIECE, SEG), BF16),
            pltpu.VMEM((ZH, CORES, OWNERS, PIECE, SEG), BF16),
            pltpu.VMEM((ZH, Y, BLK, PANEL), BF16),
            pltpu.VMEM((ROWS, PANEL), F32),
            dma((164,)), dma((ZH,)), dma, dma, dma((2, 2, 3)), dma((2, 4)), dma((2, 4)),
            dma((4,)), dma((4,)), dma((4,)), dma((4,)), dma((4,)), dma((4,)),
        ],
        compiler_params=pltpu.CompilerParams(
            collective_id=0, has_side_effects=True, vmem_limit_bytes=48 * 1024 * 1024
        ),
        name="panel_update",
    )(
        counts, col_index, barrier.reshape(-1, BW), border,
        inverse.reshape(Y, ZH, BLK, PANEL), slab,
    )


def solution(mesh):
    return jax.shard_map(
        body,
        mesh=mesh,
        in_specs=(P("scen", "row", None), P("scen", None), P(), P(), P(), P("row", "scen")),
        out_specs=P("row", "scen"),
        check_vma=False,
    )
```

time: 684 us -> 96.5 us (0.14)
  the two profiles are of different devices: /device:TPU:33 before, /device:TPU:81 now
where the time goes in v1:
time: 96.5 us; the launch traced here: 96.2 us
  Pallas kernels  89.7 us (93%)
  local copies, waits for them, and re-layouts  6.44 us (7%)
    pallas_call x1, Pallas kernels, body(): pl.pallas_call(kernel, out_shape=jax.ShapeDtypeStruct(slab.shape, slab.dt...  89.7 us
    unnamed x13, local copies, waits for them, and re-layouts  6.44 us

profile of v1, /device:TPU:81, one launch (start us, length us, event | category | flops | bytes accessed | tf_op | source)
XLA Modules:
  0.0 96.2 jit_solution(2388711308912847350)
XLA Ops:
  0.0 0.0 copy-start
  0.0 1.6 %copy-done = bf16[1024,1024]{1,0:T(8,128)(2,1)S(1)} copy-done((bf16[1024,1024]{1,0:T(8,128)(2,1)S(1)}, bf16[1024,1024]{1,0:T(8,128)(2,1)}, u32[]{:S(2)}) %copy-start) | copy-done | bytes 2097176
  1.6 0.0 copy-start.1
  1.6 1.2 %copy-done.1 = bf16[16,256,128]{2,1,0:T(8,128)(2,1)S(1)} copy-done((bf16[16,256,128]{2,1,0:T(8,128)(2,1)S(1)}, bf16[16,256,128]{2,1,0:T(8,128)(2,1)}, u32[]{:S(2)}) %copy-start.1) | copy-done | bytes 1048600
  2.8 0.0 copy-start.2
  2.8 0.9 copy-done.2
  3.7 0.0 copy-start.3
  3.7 0.7 copy-done.3
  4.4 0.0 copy-start.4
  4.4 0.7 copy-done.4
  5.1 0.0 copy-start.5
  5.1 0.7 copy-done.5
  5.8 89.7 %panel_update.1 = f32[256,128]{1,0:T(8,128)S(1)} custom-call(s32[32]{0:T(128)S(1)} %copy-done.5, s32[16,128]{1,0:T(8,128)S(1)} %copy-done.4, f32[32,128]{1,0:T(8,128)S(1)} %bitcast.3, bf16[16,256,128]{2,1,0:T(8,128)(2,1)S(1)} %copy-done.1, bf16[4,4,64,1024]{3,2,1,0:T(8,128)(2,1)S(1)} %bitcast.2, f32[256,128]{1,0:T(8,128)S(1)} %copy-done.2), custom_call_target="tpu_custom_call" | custom-call | tf_op jit(solution)/shard_map/panel_update/pallas_call | solution.py:336
  95.5 0.7 copy.8
Async XLA Ops:
  0.0 1.6 %copy-start = (bf16[1024,1024]{1,0:T(8,128)(2,1)S(1)}, bf16[1024,1024]{1,0:T(8,128)(2,1)}, u32[]{:S(2)}) copy-start(bf16[1024,1024]{1,0:T(8,128)(2,1)} %param.10) | copy-start | bytes 6291460
  1.6 1.2 %copy-start.1 = (bf16[16,256,128]{2,1,0:T(8,128)(2,1)S(1)}, bf16[16,256,128]{2,1,0:T(8,128)(2,1)}, u32[]{:S(2)}) copy-start(bf16[16,256,128]{2,1,0:T(8,128)(2,1)} %border.1) | copy-start | bytes 3145732
  2.8 0.9 copy-start.2
  3.7 0.7 copy-start.3
  4.4 0.7 copy-start.4
  5.1 0.7 copy-start.5

commit v2 on v1

--- a/solution.py
+++ b/solution.py
@@ -21,10 +21,10 @@
 
 
 def kernel(
-    counts, index, table, border, inverse, slab, out,
-    kept, parcels, arrived, h0, h1, part, xin, xsum, zin, own, zg, full, trail, inv, acc,
-    send_sems, inv_sem, head_sem, body_sem, z_sems, y_sems, c_sems,
-    xr_sems, zr_sems, zg_sems, xg_sems, tz_sems, tc_sems,
+    counts_in, index_in, table_in, border_in, inverse, slab_in, out,
+    counts, index, table, border, slab, kept, parcels, arrived, h0, h1, part, xin, xsum, zin, own, zg, full, trail, inv, acc,
+    send_sems, in_sems, inv_sem, head_sem, body_sem, z_sems, y_sems, c_sems,
+    xr_sems, zr_sems, zg_sems, xg_sems, tz_sems, tc_sems, below_sem, above_sem,
 ):
     sc, rw = lax.axis_index("scen"), lax.axis_index("row")
     x, zl = sc % X, sc // X
@@ -62,14 +62,32 @@
     def arrive(ref, sem):
         pltpu.make_async_copy(ref, ref, sem).wait()
 
+    loads = [
+        pltpu.make_async_copy(source, target, in_sems.at[n])
+        for n, (source, target) in enumerate((
+            (index_in, index), (table_in, table), (counts_in, counts),
+            (border_in.at[:, 0:SHARE], border.at[:, 0:SHARE]),
+            (border_in.at[:, SHARE:ROWS], border.at[:, SHARE:ROWS]),
+            (slab_in, slab),
+        ))
+    ]
+    for copy in loads:
+        copy.start()
+
     barrier = pltpu.get_barrier_semaphore()
     peers = [dev(x_=xp(d), c_=cc) for d in range(1, X) for cc in range(CORES)]
     peers += [dev(c_=1 - c)]
-    peers += [dev(zl_=(zl + d) % ZL) for d in range(1, ZL)]
     peers += [dev(zh_=zp(1)), dev(zh_=zp(-1))]
     peers += [dev(y_=yp(d)) for d in range(1, Y)]
+    mesh_id = pl.DeviceIdType.MESH
     for peer in peers:
-        pl.semaphore_signal(barrier, inc=1, device_id=peer, device_id_type=pl.DeviceIdType.MESH)
+        pl.semaphore_signal(barrier, inc=1, device_id=peer, device_id_type=mesh_id)
+    up, down = zl < ZL - 1, zl > 0
+    for pred, step in ((up, 1), (down, -1)):
+        @pl.when(pred)
+        def _(step=step):
+            target = dev(zl_=zl + step)
+            pl.semaphore_signal(barrier, inc=1, device_id=target, device_id_type=mesh_id)
 
     inv_copies = [
         pltpu.make_async_copy(inverse.at[:, b], inv.at[b], inv_sem.at[b]) for b in range(ZH)
@@ -77,6 +95,8 @@
     for copy in inv_copies:
         copy.start()
 
+    for copy in loads[0:3]:
+        copy.wait()
     indices = index[...]
     high, low = indices // BW, indices % BW
     weights = jnp.zeros(indices.shape, F32)
@@ -94,12 +114,14 @@
     def lanes(k):
         return slice(k * BW, (k + 1) * BW)
 
+    loads[3].wait()
     for k in range(OWN):
         h0[zh, y, c, :, lanes(k)] = scaled(k, 0, SHARE)
     for o in range(SURPLUS):
         for e in range(EXTRA):
             parcels[o, 0:SHARE, lanes(e)] = scaled(OWN + EXTRA * (o + 1) + e, 0, SHARE)
-    pl.semaphore_wait(barrier, len(peers))
+    near = up.astype(jnp.int32) + down.astype(jnp.int32)
+    pl.semaphore_wait(barrier, len(peers) + near)
 
     heads = ((h0, 0), (h1, 1))
     halves = ((0, PIECE), (PIECE, SHARE))
@@ -144,6 +166,7 @@
     for o in range(SURPLUS):
         send(parcels.at[o, 0:SHARE], arrived.at[o, 0:SHARE], head_sem, dev(x_=xp(o + 1)))
     y_start(h0, 0, 0)
+    loads[4].wait()
     for o in range(SURPLUS):
         for e in range(EXTRA):
             parcels[o, SHARE:ROWS, lanes(e)] = scaled(OWN + EXTRA * (o + 1) + e, SHARE, ROWS)
@@ -162,12 +185,19 @@
     kept[0:SHARE, W0 : W0 + W1] = extra_heads
     z_start(h1, 1)
     y_start(h1, 1, 0)
+
+    for wait_if, send_if, step, sem in ((down, up, 1, below_sem), (up, down, -1, above_sem)):
+        @pl.when(wait_if)
+        def _(sem=sem):
+            pl.semaphore_wait(sem, 1)
+
+        @pl.when(send_if)
+        def _(step=step, sem=sem):
+            target = dev(zl_=zl + step)
+            pl.semaphore_signal(sem, inc=1, device_id=target, device_id_type=mesh_id)
+
     for k in range(OWN):
         kept[:, lanes(k)] = scaled(k, 0, ROWS)
-    arrive(arrived.at[:, SHARE:ROWS], body_sem)
-    kept[SHARE:ROWS, W0 : W0 + W1] = with_parcels(SHARE, ROWS)
-    c_start(h0, 0, 0)
-    c_start(h1, 1, 0)
 
     left = x // CORES
     upper = x % CORES
@@ -227,25 +257,23 @@
         keep(zg.at[n], dst, xg_sems.at[n], left == c)
 
     on_line = y == zl // ZH
-    lag = (zh - zl % ZH + ZH) % ZH
-
-    def t_segment(n):
-        return (zl % ZH + origins[n] + ZH) % ZH
-
-    def t_source(n):
-        source = jnp.logical_and(on_line, lag == 0)
-        dst = trail.at[t_segment(n), c]
-        send(zg.at[n], dst, tz_sems.at[n], dev(zh_=zp(1)), source)
-        send(zg.at[n], dst, tz_sems.at[n], dev(zh_=zp(-1)), source)
-        keep(zg.at[n], dst, tz_sems.at[n], source)
+    source = jnp.logical_and(on_line, zh == zl % ZH)
+
+    def t_segment(n, origin):
+        return (origin + origins[n] + ZH) % ZH
+
+    def t_send(n):
+        pred = jnp.logical_and(owner, y < ZL // ZH)
+        dst = trail.at[t_segment(n, zh), c, seat]
+        for d in (2, 1, 3):
+            send(own.at[n], dst, tz_sems.at[n], dev(zl_=(y * ZH + zh) % ZL, zh_=zp(d)), pred)
+
+    def t_keep(n):
+        keep(zg.at[n], trail.at[t_segment(n, zh), c], tz_sems.at[n], source)
 
     def t_spread(n):
-        ref = trail.at[t_segment(n), c]
+        ref = trail.at[t_segment(n, zl % ZH), c]
         arrive(ref, tz_sems.at[n])
-        for a, step, at in ((0, 1, 1), (1, -1, 3)):
-            cut = trail.at[t_segment(n), c, 2 * a : 2 * a + 2]
-            pred = jnp.logical_and(on_line, lag == at)
-            send(cut, cut, tz_sems.at[n], dev(zh_=zp(step)), pred)
         for d in (1, 3, 2):
             send(ref, ref, tz_sems.at[n], dev(y_=yp(d)), on_line)
         send(ref, ref, tc_sems.at[n], dev(c_=1 - c))
@@ -264,55 +292,55 @@
         else:
             acc[...] += step
 
+    def relay(h, k):
+        z_relay(h, k)
+        z_rest(h, k, -1)
+        y_start(h, k, 1)
+        z_rest(h, k, 1)
+        y_start(h, k, 2)
+
+    c_start(h0, 0, 0)
+    c_start(h1, 1, 0)
+    relay(h0, 0)
+    arrive(arrived.at[:, SHARE:ROWS], body_sem)
+    kept[SHARE:ROWS, W0 : W0 + W1] = with_parcels(SHARE, ROWS)
     product(0)
-    z_relay(h0, 0)
-    z_rest(h0, 0, -1)
-    y_start(h0, 0, 1)
-    z_rest(h0, 0, 1)
-    y_start(h0, 0, 2)
+    relay(h1, 1)
     x_reduce(0)
-    z_relay(h1, 1)
-    z_rest(h1, 1, -1)
-    y_start(h1, 1, 1)
-    z_rest(h1, 1, 1)
-    y_start(h1, 1, 2)
-    c_start(h0, 0, 1)
-    c_start(h0, 0, 2)
-    c_start(h1, 1, 1)
-    c_start(h1, 1, 2)
+    for n in (1, 2):
+        c_start(h0, 0, n)
+        c_start(h1, 1, n)
     product(1)
     product(2)
+    for h, k in heads:
+        z_rest(h, k, 2)
+        y_start(h, k, 3)
     z_reduce(0)
-    z_rest(h0, 0, 2)
-    y_start(h0, 0, 3)
-    z_rest(h1, 1, 2)
-    y_start(h1, 1, 3)
+    t_send(0)
     x_reduce(1)
     x_reduce(2)
     c_start(h0, 0, 3)
     c_start(h1, 1, 3)
     product(3)
-    x_gather(0)
-    t_source(0)
-    z_reduce(1)
-    z_reduce(2)
+    for n in (1, 2):
+        z_reduce(n)
+        t_send(n)
     x_reduce(3)
-    for n in (1, 2):
+    for n in range(3):
         x_gather(n)
-        t_source(n)
+        t_keep(n)
     z_reduce(3)
+    t_send(3)
     for n in range(3):
         finish_part(n)
     x_gather(3)
-    t_source(3)
-    t_spread(0)
-    t_spread(1)
-    t_spread(2)
+    t_keep(3)
+    for n in range(4):
+        t_spread(n)
     finish_part(3)
     finished = acc[...].astype(BF16)
-    t_spread(3)
     for n in range(4):
-        arrive(trail.at[t_segment(n), 1 - c], tc_sems.at[n])
+        arrive(trail.at[t_segment(n, zl % ZH), 1 - c], tc_sems.at[n])
     segments = [trail[b].reshape(2 * BLK, SEG).astype(F32) for b in range(ZH)]
     update = jnp.zeros(out.shape, F32)
     for yy in range(Y):
@@ -321,6 +349,7 @@
             columns = jnp.concatenate([segments[2 * pair][:, cut], segments[2 * pair + 1][:, cut]], axis=1)
             at = (yy * (ZH // 2) + pair) * BW
             update = update + nt_dot(finished[:, at : at + BW], columns.astype(BF16))
+    loads[5].wait()
     out[...] = slab[...] - update
 
     for pred, copy in pending:
@@ -336,12 +365,14 @@
     return pl.pallas_call(
         kernel,
         out_shape=jax.ShapeDtypeStruct(slab.shape, slab.dtype),
-        in_specs=[
-            pl.BlockSpec(memory_space=pltpu.SMEM), vmem, vmem, vmem,
-            pl.BlockSpec(memory_space=pl.ANY), vmem,
-        ],
+        in_specs=[pl.BlockSpec(memory_space=pl.ANY)] * 6,
         out_specs=vmem,
         scratch_shapes=[
+            pltpu.SMEM(counts.shape, counts.dtype),
+            pltpu.VMEM(col_index.shape, col_index.dtype),
+            pltpu.VMEM((barrier.shape[0] // BW, BW), barrier.dtype),
+            pltpu.VMEM(border.shape, border.dtype),
+            pltpu.VMEM(slab.shape, slab.dtype),
             pltpu.VMEM((ROWS, W0 + W1), BF16),
             pltpu.VMEM((SURPLUS, ROWS, W1), BF16),
             pltpu.VMEM((SURPLUS, ROWS, W1), BF16),
@@ -357,11 +388,12 @@
             pltpu.VMEM((ZH, CORES, OWNERS, PIECE, SEG), BF16),
             pltpu.VMEM((ZH, Y, BLK, PANEL), BF16),
             pltpu.VMEM((ROWS, PANEL), F32),
-            dma((164,)), dma((ZH,)), dma, dma, dma((2, 2, 3)), dma((2, 4)), dma((2, 4)),
+            dma((164,)), dma((6,)), dma((ZH,)), dma, dma, dma((2, 2, 3)), dma((2, 4)), dma((2, 4)),
             dma((4,)), dma((4,)), dma((4,)), dma((4,)), dma((4,)), dma((4,)),
+            pltpu.SemaphoreType.REGULAR, pltpu.SemaphoreType.REGULAR,
         ],
         compiler_params=pltpu.CompilerParams(
-            collective_id=0, has_side_effects=True, vmem_limit_bytes=48 * 1024 * 1024
+            collective_id=0, has_side_effects=True, vmem_limit_bytes=67043328
         ),
         name="panel_update",
     )(

time: 96.5 us -> 90.9 us (0.942)
  local copies, waits for them, and re-layouts: 6.44 us -> 1.57 us
    unnamed x13 -> x1, local copies, waits for them, and re-layouts: 6.44 us -> 1.57 us
where the time goes in v2:
time: 90.9 us; the launch traced here: 90.7 us
  Pallas kernels  89.1 us (98%)
  local copies, waits for them, and re-layouts  1.57 us (2%)
    pallas_call x1, Pallas kernels, body(): pl.pallas_call(kernel, out_shape=jax.ShapeDtypeStruct(slab.shape, slab.dt...  89.1 us

profile of v2, /device:TPU:81, one launch (start us, length us, event | category | flops | bytes accessed | tf_op | source)
XLA Modules:
  0.0 90.7 jit_solution(17354011101679673829)
XLA Ops:
  0.0 89.1 %panel_update.1 = f32[256,128]{1,0:T(8,128)} custom-call(s32[32]{0:T(128)} %counts_in.1, s32[16,128]{1,0:T(8,128)} %index_in.1, f32[32,128]{1,0:T(8,128)} %bitcast.3, bf16[16,256,128]{2,1,0:T(8,128)(2,1)} %border_in.1, bf16[4,4,64,1024]{3,2,1,0:T(8,128)(2,1)} %bitcast.2, f32[256,128]{1,0:T(8,128)} %slab_in.1), custom_call_target="tpu_custom_call" | custom-call | tf_op jit(solution)/shard_map/panel_update/pallas_call | solution.py:365
  89.1 1.6 %copy.8 = f32[256,128]{1,0:T(8,128)} copy(f32[256,128]{1,0:T(8,128)} %panel_update.1) | data formatting | bytes 262144

commit v3 on v2

--- a/solution.py
+++ b/solution.py
@@ -186,15 +186,27 @@
     z_start(h1, 1)
     y_start(h1, 1, 0)
 
-    for wait_if, send_if, step, sem in ((down, up, 1, below_sem), (up, down, -1, above_sem)):
-        @pl.when(wait_if)
-        def _(sem=sem):
+    def token(step, sem):
+        first, last = (0, ZL - 1) if step == 1 else (ZL - 1, 0)
+
+        @pl.when(zl != first)
+        def _():
             pl.semaphore_wait(sem, 1)
 
-        @pl.when(send_if)
-        def _(step=step, sem=sem):
+        @pl.when(zl != last)
+        def _():
             target = dev(zl_=zl + step)
             pl.semaphore_signal(sem, inc=1, device_id=target, device_id_type=mesh_id)
+
+    @pl.when(zl < ZL // 2)
+    def _():
+        token(1, below_sem)
+        token(-1, above_sem)
+
+    @pl.when(zl >= ZL // 2)
+    def _():
+        token(-1, above_sem)
+        token(1, below_sem)
 
     for k in range(OWN):
         kept[:, lanes(k)] = scaled(k, 0, ROWS)
@@ -302,25 +314,25 @@
     c_start(h0, 0, 0)
     c_start(h1, 1, 0)
     relay(h0, 0)
+    relay(h1, 1)
     arrive(arrived.at[:, SHARE:ROWS], body_sem)
     kept[SHARE:ROWS, W0 : W0 + W1] = with_parcels(SHARE, ROWS)
     product(0)
-    relay(h1, 1)
-    x_reduce(0)
     for n in (1, 2):
         c_start(h0, 0, n)
         c_start(h1, 1, n)
     product(1)
     product(2)
+    x_reduce(0)
     for h, k in heads:
         z_rest(h, k, 2)
         y_start(h, k, 3)
-    z_reduce(0)
-    t_send(0)
     x_reduce(1)
     x_reduce(2)
     c_start(h0, 0, 3)
     c_start(h1, 1, 3)
+    z_reduce(0)
+    t_send(0)
     product(3)
     for n in (1, 2):
         z_reduce(n)
@@ -335,9 +347,10 @@
         finish_part(n)
     x_gather(3)
     t_keep(3)
-    for n in range(4):
+    for n in range(3):
         t_spread(n)
     finish_part(3)
+    t_spread(3)
     finished = acc[...].astype(BF16)
     for n in range(4):
         arrive(trail.at[t_segment(n, zl % ZH), 1 - c], tc_sems.at[n])

time: 90.9 us -> 87.6 us (0.964)
  Pallas kernels: 89.1 us -> 85.8 us
    pallas_call x1, Pallas kernels: 89.1 us -> 85.8 us  [body(): pl.pallas_call(kernel, out_shape=jax.ShapeDtypeStruct(slab.shape, slab.dt...]
where the time goes in v3:
time: 87.6 us; the launch traced here: 87.4 us
  Pallas kernels  85.8 us (98%)
  local copies, waits for them, and re-layouts  1.57 us (2%)
    pallas_call x1, Pallas kernels, body(): pl.pallas_call(kernel, out_shape=jax.ShapeDtypeStruct(slab.shape, slab.dt...  85.8 us

profile of v3, /device:TPU:81, one launch (start us, length us, event | category | flops | bytes accessed | tf_op | source)
XLA Modules:
  0.0 87.4 jit_solution(13115413203439233664)
XLA Ops:
  0.0 85.8 %panel_update.1 = f32[256,128]{1,0:T(8,128)} custom-call(s32[32]{0:T(128)} %counts_in.1, s32[16,128]{1,0:T(8,128)} %index_in.1, f32[32,128]{1,0:T(8,128)} %bitcast.3, bf16[16,256,128]{2,1,0:T(8,128)(2,1)} %border_in.1, bf16[4,4,64,1024]{3,2,1,0:T(8,128)(2,1)} %bitcast.2, f32[256,128]{1,0:T(8,128)} %slab_in.1), custom_call_target="tpu_custom_call" | custom-call | tf_op jit(solution)/shard_map/panel_update/pallas_call | solution.py:378
  85.8 1.6 %copy.8 = f32[256,128]{1,0:T(8,128)} copy(f32[256,128]{1,0:T(8,128)} %panel_update.1) | data formatting | bytes 262144

commit v4 on v3

v4 whole, which is shorter than its diff:
```python
import jax
import jax.numpy as jnp
from jax import lax
from jax.experimental import pallas as pl
from jax.experimental.pallas import tpu as pltpu
from jax.sharding import PartitionSpec as P

X, ZL, Y, ZH, CORES = 4, 8, 4, 4, 2
OWN, EXTRA, SURPLUS = 4, 3, 3
BW = 128
W0, W1 = OWN * BW, EXTRA * BW
ROWS, SHARE, PANEL, HALF = 256, 32, 1024, 128
SEG = PANEL // ZH
HELD = Y * CORES * ROWS
OWNER_OF = (3, 4, 2, 5)
GROUPS = ((0, 3), (3, 4))
F32, BF16 = jnp.float32, jnp.bfloat16


def nt_dot(a, b):
    return lax.dot_general(a, b, (((1,), (1,)), ((), ())), preferred_element_type=F32)


def tn_dot(a, b):
    return lax.dot_general(a, b, (((0,), (0,)), ((), ())), preferred_element_type=F32)


def kernel(
    counts_in, index_in, table_in, border_in, inverse, slab_in, out,
    counts, index, table, border, slab, parcels, arrived, s0, s1, h0, h1,
    part, xin, xsum, zin, own, zg, full, trail, natural, inv, acc,
    send_sems, in_sems, inv_sem, head_sem, body_sem, s_sems, sc_sems, z_sems,
    xr_sems, zr_sems, zg_sems, xg_sems, tz_sems, ty_sems, tc_sems, below_sem, above_sem,
):
    sc, rw = lax.axis_index("scen"), lax.axis_index("row")
    x, zl = sc % X, sc // X
    y, zh, c = rw // (ZH * CORES), (rw // CORES) % ZH, rw % CORES
    mesh_id = pl.DeviceIdType.MESH

    def dev(x_=x, zl_=zl, y_=y, zh_=zh, c_=c):
        return (zl_ * X + x_, (y_ * ZH + zh_) * CORES + c_)

    def xp(d):
        return (x + d) % X

    def yp(d):
        return (y + d) % Y

    def zp(d):
        return (zh + d + ZH) % ZH

    pending = []

    def send(src, dst, sem, target, pred=None):
        copy = pltpu.make_async_remote_copy(
            src_ref=src, dst_ref=dst, send_sem=send_sems.at[len(pending)], recv_sem=sem,
            device_id=target, device_id_type=mesh_id,
        )
        pending.append((pred, copy))
        if pred is None:
            copy.start()
        else:
            pl.when(pred)(copy.start)

    def keep(src, dst, sem, pred):
        copy = pltpu.make_async_copy(src, dst, sem)
        pl.when(pred)(copy.start)

    def arrive(ref, sem):
        pltpu.make_async_copy(ref, ref, sem).wait()

    loads = [
        pltpu.make_async_copy(source, target, in_sems.at[n])
        for n, (source, target) in enumerate((
            (index_in, index), (table_in, table), (counts_in, counts),
            (border_in.at[:, 0:SHARE], border.at[:, 0:SHARE]),
            (border_in.at[:, SHARE:ROWS], border.at[:, SHARE:ROWS]),
            (slab_in, slab),
        ))
    ]
    for copy in loads:
        copy.start()

    barrier = pltpu.get_barrier_semaphore()
    peers = [dev(x_=xp(d)) for d in range(1, X)] + [dev(y_=yp(d)) for d in range(1, Y)]
    peers += [dev(c_=1 - c), dev(zh_=zp(1)), dev(zh_=zp(-1))]
    for peer in peers:
        pl.semaphore_signal(barrier, inc=1, device_id=peer, device_id_type=mesh_id)
    up, down = zl < ZL - 1, zl > 0
    for pred, step in ((up, 1), (down, -1)):
        @pl.when(pred)
        def _(step=step):
            target = dev(zl_=zl + step)
            pl.semaphore_signal(barrier, inc=1, device_id=target, device_id_type=mesh_id)

    inv_copies = [
        pltpu.make_async_copy(inverse.at[:, b], inv.at[b], inv_sem.at[b]) for b in range(ZH)
    ]
    for copy in inv_copies:
        copy.start()

    for copy in loads[0:3]:
        copy.wait()
    indices = index[...]
    high, low = indices // BW, indices % BW
    weights = jnp.zeros(indices.shape, F32)
    for h in range(table.shape[0]):
        row = jnp.broadcast_to(table[h : h + 1, :], indices.shape)
        picked = jnp.take_along_axis(row, low, axis=1, mode="promise_in_bounds")
        weights = jnp.where(high == h, picked, weights)
    slots = lax.broadcasted_iota(jnp.int32, indices.shape, 0)
    weights = jnp.where(slots < counts[sc], weights, 0.0)

    def scaled(k, first, last):
        rows = border[k, first:last, :].astype(F32)
        return (rows * weights[k : k + 1, :]).astype(BF16)

    def lanes(k):
        return slice(k * BW, (k + 1) * BW)

    loads[3].wait()
    for k in range(OWN):
        h0[zh, :, lanes(k)] = scaled(k, 0, SHARE)
    for o in range(SURPLUS):
        for e in range(EXTRA):
            parcels[o, 0:SHARE, lanes(e)] = scaled(OWN + EXTRA * (o + 1) + e, 0, SHARE)
    near = up.astype(jnp.int32) + down.astype(jnp.int32)
    pl.semaphore_wait(barrier, len(peers) + near)

    heads = ((h0, 0), (h1, 1))
    cuts = ((0, SHARE // 2), (SHARE // 2, SHARE))

    def z_start(h, k):
        for a, step in ((0, 1), (1, -1), (1, 1), (0, -1)):
            lo, hi = cuts[a]
            ref = h.at[zh, lo:hi]
            send(ref, ref, z_sems.at[k, a, 0 if step == 1 else 1], dev(zh_=zp(step)))

    def z_relay(h, k):
        for a, step in ((0, 1), (1, -1)):
            lo, hi = cuts[a]
            ref = h.at[zp(-step), lo:hi]
            arrive(ref, z_sems.at[k, a, 0 if step == 1 else 1])
            send(ref, ref, z_sems.at[k, a, 2], dev(zh_=zp(step)))

    def z_rest(h, k, origin):
        if origin == 2:
            for a in range(2):
                lo, hi = cuts[a]
                arrive(h.at[zp(2), lo:hi], z_sems.at[k, a, 2])
        else:
            a, way = (1, 0) if origin == -1 else (0, 1)
            lo, hi = cuts[a]
            arrive(h.at[zp(origin), lo:hi], z_sems.at[k, a, way])

    origins = (0, -1, 1, 2)

    def s_start(s, k):
        ref = s.at[c, :, y]
        for d in (2, 1, 3):
            send(ref, ref, s_sems.at[k], dev(y_=yp(d)))

    def s_cross(s, k):
        arrive(s.at[c, :, 0 : Y - 1], s_sems.at[k])
        send(s.at[c], s.at[c], sc_sems.at[k], dev(c_=1 - c))

    z_start(h0, 0)
    for o in range(SURPLUS):
        send(parcels.at[o, 0:SHARE], arrived.at[o, 0:SHARE], head_sem, dev(x_=xp(o + 1)))
    loads[4].wait()
    for o in range(SURPLUS):
        for e in range(EXTRA):
            parcels[o, SHARE:ROWS, lanes(e)] = scaled(OWN + EXTRA * (o + 1) + e, SHARE, ROWS)
        send(parcels.at[o, SHARE:ROWS], arrived.at[o, SHARE:ROWS], body_sem, dev(x_=xp(o + 1)))

    def with_parcels(first, last):
        mine = [scaled(OWN + e, first, last) for e in range(EXTRA)]
        total = jnp.concatenate(mine, axis=1)
        for o in range(SURPLUS):
            total = total + arrived[o, first:last, :]
        return total

    arrive(arrived.at[:, 0:SHARE], head_sem)
    h1[zh] = with_parcels(0, SHARE)
    z_start(h1, 1)
    for k in range(OWN):
        for half in range(2):
            s0[c, half, y, :, lanes(k)] = scaled(k, half * HALF, (half + 1) * HALF)
    s_start(s0, 0)

    def token(step, sem):
        first, last = (0, ZL - 1) if step == 1 else (ZL - 1, 0)

        @pl.when(zl != first)
        def _():
            pl.semaphore_wait(sem, 1)

        @pl.when(zl != last)
        def _():
            target = dev(zl_=zl + step)
            pl.semaphore_signal(sem, inc=1, device_id=target, device_id_type=mesh_id)

    @pl.when(zl < ZL // 2)
    def _():
        token(1, below_sem)
        token(-1, above_sem)

    @pl.when(zl >= ZL // 2)
    def _():
        token(-1, above_sem)
        token(1, below_sem)

    group_of = {0: slice(*GROUPS[0]), 1: slice(*GROUPS[1])}

    def product(g):
        first, last = GROUPS[g]
        at = [zp(origins[n]) for n in range(first, last)]
        a = jnp.concatenate([h0[z] for z in at], axis=0)
        b = jnp.concatenate([h1[z] for z in at], axis=0)
        block = nt_dot(a, s0[...].reshape(HELD, W0)) + nt_dot(b, s1[...].reshape(HELD, W1))
        block = block.astype(BF16)
        wide = HELD // X
        for n in range(first, last):
            for t in range(X):
                rows = slice((n - first) * SHARE, (n - first + 1) * SHARE)
                part[n, t] = block[rows, t * wide : (t + 1) * wide]
        for d in (2, 1, 3):
            send(part.at[group_of[g], xp(d)], xin.at[group_of[g], x], xr_sems.at[g], dev(x_=xp(d)))
        copy = pltpu.make_async_copy(part.at[group_of[g], x], xin.at[group_of[g], x], xr_sems.at[g])
        copy.start()

    def x_reduce(g):
        arrive(xin.at[group_of[g]], xr_sems.at[g])
        for n in range(*GROUPS[g]):
            total = xin[n, 0].astype(F32)
            for s in range(1, X):
                total = total + xin[n, s].astype(F32)
            total = total.astype(BF16)
            for j in range(Y):
                xsum[n, j] = total[:, j * HALF : (j + 1) * HALF]
        for j in range(Y):
            here = zl == OWNER_OF[j]
            src, dst = xsum.at[group_of[g], j], zin.at[group_of[g], zl]
            send(src, dst, zr_sems.at[g], dev(zl_=OWNER_OF[j]), jnp.logical_not(here))
            keep(src, dst, zr_sems.at[g], here)

    owner = jnp.logical_and(zl >= min(OWNER_OF), zl <= max(OWNER_OF))
    seat = jnp.where(zl == OWNER_OF[0], 0, jnp.where(zl == OWNER_OF[1], 1, jnp.where(zl == OWNER_OF[2], 2, 3)))
    gives = jnp.logical_and(owner, seat < ZL // ZH)
    goes_to = (seat * ZH + zh) % ZL

    def z_reduce(g):
        @pl.when(owner)
        def _():
            arrive(zin.at[group_of[g]], zr_sems.at[g])
            for n in range(*GROUPS[g]):
                total = zin[n, 0].astype(F32)
                for s in range(1, ZL):
                    total = total + zin[n, s].astype(F32)
                own[n] = total.astype(BF16)

        src = own.at[group_of[g]]
        for d in (2, 1, 3):
            send(src, trail.at[group_of[g], y, c], tz_sems.at[g], dev(zl_=goes_to, zh_=zp(d)), gives)
        for d in range(1, ZL):
            send(src, zg.at[group_of[g], seat], zg_sems.at[g], dev(zl_=(zl + d) % ZL), owner)
        keep(src, zg.at[group_of[g], seat], zg_sems.at[g], owner)

    def gather(g):
        arrive(zg.at[group_of[g]], zg_sems.at[g])
        keep(zg.at[group_of[g], zl // ZH], trail.at[group_of[g], y, c], tz_sems.at[g], zh == zl % ZH)
        side = pl.ds(pl.multiple_of((x % 2) * HALF, HALF), HALF)
        dst = full.at[group_of[g], y * CORES + c, :, side]
        for j in range(Y):
            src = zg.at[group_of[g], j]
            for d in range(X):
                target = dev(x_=xp(d), y_=j, c_=x // 2)
                if d:
                    send(src, dst, xg_sems.at[g], target)
                else:
                    here = jnp.logical_and(y == j, c == x // 2)
                    send(src, dst, xg_sems.at[g], target, jnp.logical_not(here))
                    keep(src, dst, xg_sems.at[g], here)

    def spread(g):
        ref = trail.at[group_of[g], y, c]
        arrive(ref, tz_sems.at[g])
        for d in (2, 1, 3):
            for cc in (c, 1 - c):
                send(ref, ref, ty_sems.at[g], dev(y_=yp(d), c_=cc))
        send(ref, ref, tc_sems.at[g], dev(c_=1 - c))

    def place(g):
        arrive(trail.at[group_of[g], 0 : Y - 1], ty_sems.at[g])
        arrive(trail.at[group_of[g], 0, 0], tc_sems.at[g])
        for n in range(*GROUPS[g]):
            natural[:, (zl % ZH + origins[n] + ZH) % ZH] = trail[n]

    def finish(g):
        arrive(full.at[group_of[g]], xg_sems.at[g])
        for n in range(*GROUPS[g]):
            step = tn_dot(full[n].reshape(SEG, ROWS), inv[zp(origins[n])].reshape(SEG, PANEL))
            if n == 0:
                acc[...] = step
            else:
                acc[...] += step

    def relay(h, k):
        z_relay(h, k)
        z_rest(h, k, -1)
        z_rest(h, k, 1)

    relay(h0, 0)
    arrive(arrived.at[:, SHARE:ROWS], body_sem)
    for half in range(2):
        s1[c, half, y] = with_parcels(half * HALF, (half + 1) * HALF)
    s_start(s1, 1)
    relay(h1, 1)
    s_cross(s0, 0)
    s_cross(s1, 1)
    for s, k in ((s0, 0), (s1, 1)):
        arrive(s.at[1 - c], sc_sems.at[k])
    product(0)
    for h, k in heads:
        z_rest(h, k, 2)
    product(1)
    x_reduce(0)
    x_reduce(1)
    z_reduce(0)
    z_reduce(1)
    for copy in inv_copies:
        copy.wait()
    gather(0)
    gather(1)
    spread(0)
    finish(0)
    place(0)
    finish(1)
    finished = acc[...].astype(BF16)
    spread(1)
    place(1)
    loads[5].wait()
    update = jnp.dot(finished, natural[...].reshape(PANEL, HALF), preferred_element_type=F32)
    out[...] = slab[...] - update

    for pred, copy in pending:
        if pred is None:
            copy.wait_send()
        else:
            pl.when(pred)(copy.wait_send)


def body(border, col_index, barrier, counts, inverse, slab):
    dma = pltpu.SemaphoreType.DMA
    wide = HELD // X
    return pl.pallas_call(
        kernel,
        out_shape=jax.ShapeDtypeStruct(slab.shape, slab.dtype),
        in_specs=[pl.BlockSpec(memory_space=pl.ANY)] * 6,
        out_specs=pl.BlockSpec(memory_space=pltpu.VMEM),
        scratch_shapes=[
            pltpu.SMEM(counts.shape, counts.dtype),
            pltpu.VMEM(col_index.shape, col_index.dtype),
            pltpu.VMEM((barrier.shape[0] // BW, BW), barrier.dtype),
            pltpu.VMEM(border.shape, border.dtype),
            pltpu.VMEM(slab.shape, slab.dtype),
            pltpu.VMEM((SURPLUS, ROWS, W1), BF16),
            pltpu.VMEM((SURPLUS, ROWS, W1), BF16),
            pltpu.VMEM((CORES, 2, Y, HALF, W0), BF16),
            pltpu.VMEM((CORES, 2, Y, HALF, W1), BF16),
            pltpu.VMEM((ZH, SHARE, W0), BF16),
            pltpu.VMEM((ZH, SHARE, W1), BF16),
            pltpu.VMEM((ZH, X, SHARE, wide), BF16),
            pltpu.VMEM((ZH, X, SHARE, wide), BF16),
            pltpu.VMEM((ZH, Y, SHARE, HALF), BF16),
            pltpu.VMEM((ZH, ZL, SHARE, HALF), BF16),
            pltpu.VMEM((ZH, SHARE, HALF), BF16),
            pltpu.VMEM((ZH, Y, SHARE, HALF), BF16),
            pltpu.VMEM((ZH, Y * CORES, SHARE, ROWS), BF16),
            pltpu.VMEM((ZH, Y, CORES, SHARE, HALF), BF16),
            pltpu.VMEM((Y, ZH, CORES, SHARE, HALF), BF16),
            pltpu.VMEM((ZH, Y, CORES * SHARE, PANEL), BF16),
            pltpu.VMEM((ROWS, PANEL), F32),
            dma((128,)), dma((6,)), dma((ZH,)), dma, dma, dma((2,)), dma((2,)), dma((2, 2, 3)),
            dma((2,)), dma((2,)), dma((2,)), dma((2,)), dma((2,)), dma((2,)), dma((2,)),
            pltpu.SemaphoreType.REGULAR, pltpu.SemaphoreType.REGULAR,
        ],
        compiler_params=pltpu.CompilerParams(
            collective_id=0, has_side_effects=True, vmem_limit_bytes=67043328
        ),
        name="panel_update",
    )(
        counts, col_index, barrier.reshape(-1, BW), border,
        inverse.reshape(Y, ZH, CORES * SHARE, PANEL), slab,
    )


def solution(mesh):
    return jax.shard_map(
        body,
        mesh=mesh,
        in_specs=(P("scen", "row", None), P("scen", None), P(), P(), P(), P("row", "scen")),
        out_specs=P("row", "scen"),
        check_vma=False,
    )
```

time: 87.6 us -> 92 us (1.050)
  the two profiles are of different devices: /device:TPU:81 before, /device:TPU:1 now
where the time goes in v4:
time: 92 us; the launch traced here: 91.8 us
  Pallas kernels  90.3 us (98%)
  local copies, waits for them, and re-layouts  1.57 us (2%)
    pallas_call x1, Pallas kernels, body(): pl.pallas_call(kernel, out_shape=jax.ShapeDtypeStruct(slab.shape, slab.dt...  90.3 us

profile of v4, /device:TPU:1, one launch (start us, length us, event | category | flops | bytes accessed | tf_op | source)
XLA Modules:
  0.0 91.8 jit_solution(3169791360499413298)
XLA Ops:
  0.0 90.3 %panel_update.1 = f32[256,128]{1,0:T(8,128)} custom-call(s32[32]{0:T(128)} %counts_in.1, s32[16,128]{1,0:T(8,128)} %index_in.1, f32[32,128]{1,0:T(8,128)} %bitcast.3, bf16[16,256,128]{2,1,0:T(8,128)(2,1)} %border_in.1, bf16[4,4,64,1024]{3,2,1,0:T(8,128)(2,1)} %bitcast.2, f32[256,128]{1,0:T(8,128)} %slab_in.1), custom_call_target="tpu_custom_call" | custom-call | tf_op jit(solution)/shard_map/panel_update/pallas_call | solution.py:356
  90.3 1.6 %copy.8 = f32[256,128]{1,0:T(8,128)} copy(f32[256,128]{1,0:T(8,128)} %panel_update.1) | data formatting | bytes 262144

commit v5 on v4

--- a/solution.py
+++ b/solution.py
@@ -11,14 +11,9 @@
 W0, W1 = OWN * BW, EXTRA * BW
 ROWS, SHARE, PANEL, HALF = 256, 32, 1024, 128
 SEG = PANEL // ZH
-HELD = Y * CORES * ROWS
 OWNER_OF = (3, 4, 2, 5)
 GROUPS = ((0, 3), (3, 4))
 F32, BF16 = jnp.float32, jnp.bfloat16
-
-
-def nt_dot(a, b):
-    return lax.dot_general(a, b, (((1,), (1,)), ((), ())), preferred_element_type=F32)
 
 
 def tn_dot(a, b):
@@ -29,8 +24,8 @@
     counts_in, index_in, table_in, border_in, inverse, slab_in, out,
     counts, index, table, border, slab, parcels, arrived, s0, s1, h0, h1,
     part, xin, xsum, zin, own, zg, full, trail, natural, inv, acc,
-    send_sems, in_sems, inv_sem, head_sem, body_sem, s_sems, sc_sems, z_sems,
-    xr_sems, zr_sems, zg_sems, xg_sems, tz_sems, ty_sems, tc_sems, below_sem, above_sem,
+    send_sems, in_sems, inv_sem, head_sem, body_sem, s_sems, y_sems, z_sems,
+    xr_sems, zr_sems, zg_sems, xg_sems, tz_sems, tc_sems, below_sem, above_sem,
 ):
     sc, rw = lax.axis_index("scen"), lax.axis_index("row")
     x, zl = sc % X, sc // X
@@ -120,10 +115,17 @@
 
     loads[3].wait()
     for k in range(OWN):
-        h0[zh, :, lanes(k)] = scaled(k, 0, SHARE)
+        h0[zh, y, :, lanes(k)] = scaled(k, 0, SHARE)
     for o in range(SURPLUS):
         for e in range(EXTRA):
             parcels[o, 0:SHARE, lanes(e)] = scaled(OWN + EXTRA * (o + 1) + e, 0, SHARE)
+    loads[4].wait()
+    for k in range(OWN):
+        for half in range(2):
+            s0[c, half, lanes(k), :] = scaled(k, half * HALF, (half + 1) * HALF).T
+    for o in range(SURPLUS):
+        for e in range(EXTRA):
+            parcels[o, SHARE:ROWS, lanes(e)] = scaled(OWN + EXTRA * (o + 1) + e, SHARE, ROWS)
     near = up.astype(jnp.int32) + down.astype(jnp.int32)
     pl.semaphore_wait(barrier, len(peers) + near)
 
@@ -133,13 +135,13 @@
     def z_start(h, k):
         for a, step in ((0, 1), (1, -1), (1, 1), (0, -1)):
             lo, hi = cuts[a]
-            ref = h.at[zh, lo:hi]
+            ref = h.at[zh, y, lo:hi]
             send(ref, ref, z_sems.at[k, a, 0 if step == 1 else 1], dev(zh_=zp(step)))
 
     def z_relay(h, k):
         for a, step in ((0, 1), (1, -1)):
             lo, hi = cuts[a]
-            ref = h.at[zp(-step), lo:hi]
+            ref = h.at[zp(-step), y, lo:hi]
             arrive(ref, z_sems.at[k, a, 0 if step == 1 else 1])
             send(ref, ref, z_sems.at[k, a, 2], dev(zh_=zp(step)))
 
@@ -147,31 +149,46 @@
         if origin == 2:
             for a in range(2):
                 lo, hi = cuts[a]
-                arrive(h.at[zp(2), lo:hi], z_sems.at[k, a, 2])
+                arrive(h.at[zp(2), y, lo:hi], z_sems.at[k, a, 2])
         else:
             a, way = (1, 0) if origin == -1 else (0, 1)
             lo, hi = cuts[a]
-            arrive(h.at[zp(origin), lo:hi], z_sems.at[k, a, way])
+            arrive(h.at[zp(origin), y, lo:hi], z_sems.at[k, a, way])
 
     origins = (0, -1, 1, 2)
 
-    def s_start(s, k):
-        ref = s.at[c, :, y]
-        for d in (2, 1, 3):
-            send(ref, ref, s_sems.at[k], dev(y_=yp(d)))
+    def y_start(h, k, n):
+        ref = h.at[zp(origins[n]), y]
+        for d in (2, 1, 3):
+            send(ref, ref, y_sems.at[k, n], dev(y_=yp(d)))
+
+    def y_rest(n):
+        for h, k in heads:
+            arrive(h.at[zp(origins[n]), 0 : Y - 1], y_sems.at[k, n])
 
     def s_cross(s, k):
-        arrive(s.at[c, :, 0 : Y - 1], s_sems.at[k])
-        send(s.at[c], s.at[c], sc_sems.at[k], dev(c_=1 - c))
-
+        send(s.at[c], s.at[c], s_sems.at[k], dev(c_=1 - c))
+
+    def token(seat_on_line):
+        for at, step, sem in ((seat_on_line, 1, below_sem), (ZL - 1 - seat_on_line, -1, above_sem)):
+            @pl.when(zl == at)
+            def _(step=step, sem=sem):
+                if seat_on_line > 0:
+                    pl.semaphore_wait(sem, 1)
+                if seat_on_line < ZL - 1:
+                    target = dev(zl_=zl + step)
+                    pl.semaphore_signal(sem, inc=1, device_id=target, device_id_type=mesh_id)
+
+    token(0)
     z_start(h0, 0)
     for o in range(SURPLUS):
         send(parcels.at[o, 0:SHARE], arrived.at[o, 0:SHARE], head_sem, dev(x_=xp(o + 1)))
-    loads[4].wait()
+    y_start(h0, 0, 0)
+    s_cross(s0, 0)
     for o in range(SURPLUS):
-        for e in range(EXTRA):
-            parcels[o, SHARE:ROWS, lanes(e)] = scaled(OWN + EXTRA * (o + 1) + e, SHARE, ROWS)
         send(parcels.at[o, SHARE:ROWS], arrived.at[o, SHARE:ROWS], body_sem, dev(x_=xp(o + 1)))
+    token(1)
+    token(2)
 
     def with_parcels(first, last):
         mine = [scaled(OWN + e, first, last) for e in range(EXTRA)]
@@ -181,49 +198,25 @@
         return total
 
     arrive(arrived.at[:, 0:SHARE], head_sem)
-    h1[zh] = with_parcels(0, SHARE)
+    h1[zh, y] = with_parcels(0, SHARE)
     z_start(h1, 1)
-    for k in range(OWN):
-        for half in range(2):
-            s0[c, half, y, :, lanes(k)] = scaled(k, half * HALF, (half + 1) * HALF)
-    s_start(s0, 0)
-
-    def token(step, sem):
-        first, last = (0, ZL - 1) if step == 1 else (ZL - 1, 0)
-
-        @pl.when(zl != first)
-        def _():
-            pl.semaphore_wait(sem, 1)
-
-        @pl.when(zl != last)
-        def _():
-            target = dev(zl_=zl + step)
-            pl.semaphore_signal(sem, inc=1, device_id=target, device_id_type=mesh_id)
-
-    @pl.when(zl < ZL // 2)
-    def _():
-        token(1, below_sem)
-        token(-1, above_sem)
-
-    @pl.when(zl >= ZL // 2)
-    def _():
-        token(-1, above_sem)
-        token(1, below_sem)
+    y_start(h1, 1, 0)
+    token(3)
+    token(4)
 
     group_of = {0: slice(*GROUPS[0]), 1: slice(*GROUPS[1])}
 
     def product(g):
         first, last = GROUPS[g]
         at = [zp(origins[n]) for n in range(first, last)]
-        a = jnp.concatenate([h0[z] for z in at], axis=0)
-        b = jnp.concatenate([h1[z] for z in at], axis=0)
-        block = nt_dot(a, s0[...].reshape(HELD, W0)) + nt_dot(b, s1[...].reshape(HELD, W1))
-        block = block.astype(BF16)
-        wide = HELD // X
-        for n in range(first, last):
-            for t in range(X):
-                rows = slice((n - first) * SHARE, (n - first + 1) * SHARE)
-                part[n, t] = block[rows, t * wide : (t + 1) * wide]
+        a = jnp.concatenate([h0[z].reshape(BW, W0) for z in at], axis=0)
+        b = jnp.concatenate([h1[z].reshape(BW, W1) for z in at], axis=0)
+        for t in range(X):
+            block = jnp.dot(a, s0[t // 2, t % 2], preferred_element_type=F32)
+            block = block + jnp.dot(b, s1[t // 2, t % 2], preferred_element_type=F32)
+            block = block.astype(BF16).reshape(last - first, Y, SHARE, HALF)
+            for n in range(first, last):
+                part[n, t] = block[n - first]
         for d in (2, 1, 3):
             send(part.at[group_of[g], xp(d)], xin.at[group_of[g], x], xr_sems.at[g], dev(x_=xp(d)))
         copy = pltpu.make_async_copy(part.at[group_of[g], x], xin.at[group_of[g], x], xr_sems.at[g])
@@ -235,9 +228,7 @@
             total = xin[n, 0].astype(F32)
             for s in range(1, X):
                 total = total + xin[n, s].astype(F32)
-            total = total.astype(BF16)
-            for j in range(Y):
-                xsum[n, j] = total[:, j * HALF : (j + 1) * HALF]
+            xsum[n] = total.astype(BF16)
         for j in range(Y):
             here = zl == OWNER_OF[j]
             src, dst = xsum.at[group_of[g], j], zin.at[group_of[g], zl]
@@ -246,8 +237,9 @@
 
     owner = jnp.logical_and(zl >= min(OWNER_OF), zl <= max(OWNER_OF))
     seat = jnp.where(zl == OWNER_OF[0], 0, jnp.where(zl == OWNER_OF[1], 1, jnp.where(zl == OWNER_OF[2], 2, 3)))
-    gives = jnp.logical_and(owner, seat < ZL // ZH)
-    goes_to = (seat * ZH + zh) % ZL
+    gives = jnp.logical_and(owner, y < ZL // ZH)
+    goes_to = (y * ZH + zh) % ZL
+    on_line = y == zl // ZH
 
     def z_reduce(g):
         @pl.when(owner)
@@ -261,38 +253,32 @@
 
         src = own.at[group_of[g]]
         for d in (2, 1, 3):
-            send(src, trail.at[group_of[g], y, c], tz_sems.at[g], dev(zl_=goes_to, zh_=zp(d)), gives)
+            send(src, trail.at[group_of[g], seat, c], tz_sems.at[g], dev(zl_=goes_to, zh_=zp(d)), gives)
         for d in range(1, ZL):
             send(src, zg.at[group_of[g], seat], zg_sems.at[g], dev(zl_=(zl + d) % ZL), owner)
         keep(src, zg.at[group_of[g], seat], zg_sems.at[g], owner)
 
     def gather(g):
         arrive(zg.at[group_of[g]], zg_sems.at[g])
-        keep(zg.at[group_of[g], zl // ZH], trail.at[group_of[g], y, c], tz_sems.at[g], zh == zl % ZH)
+        src = zg.at[group_of[g]]
+        source = jnp.logical_and(on_line, zh == zl % ZH)
+        keep(src, trail.at[group_of[g], :, c], tz_sems.at[g], source)
         side = pl.ds(pl.multiple_of((x % 2) * HALF, HALF), HALF)
-        dst = full.at[group_of[g], y * CORES + c, :, side]
-        for j in range(Y):
-            src = zg.at[group_of[g], j]
-            for d in range(X):
-                target = dev(x_=xp(d), y_=j, c_=x // 2)
-                if d:
-                    send(src, dst, xg_sems.at[g], target)
-                else:
-                    here = jnp.logical_and(y == j, c == x // 2)
-                    send(src, dst, xg_sems.at[g], target, jnp.logical_not(here))
-                    keep(src, dst, xg_sems.at[g], here)
+        dst = full.at[group_of[g], :, c, :, side]
+        for d in (2, 1, 3):
+            send(src, dst, xg_sems.at[g], dev(x_=xp(d), c_=x // 2))
+        send(src, dst, xg_sems.at[g], dev(c_=1 - c), c != x // 2)
+        keep(src, dst, xg_sems.at[g], c == x // 2)
 
     def spread(g):
-        ref = trail.at[group_of[g], y, c]
+        ref = trail.at[group_of[g], :, c]
         arrive(ref, tz_sems.at[g])
         for d in (2, 1, 3):
-            for cc in (c, 1 - c):
-                send(ref, ref, ty_sems.at[g], dev(y_=yp(d), c_=cc))
+            send(ref, ref, tz_sems.at[g], dev(y_=yp(d)), on_line)
         send(ref, ref, tc_sems.at[g], dev(c_=1 - c))
 
     def place(g):
-        arrive(trail.at[group_of[g], 0 : Y - 1], ty_sems.at[g])
-        arrive(trail.at[group_of[g], 0, 0], tc_sems.at[g])
+        arrive(trail.at[group_of[g], :, 1 - c], tc_sems.at[g])
         for n in range(*GROUPS[g]):
             natural[:, (zl % ZH + origins[n] + ZH) % ZH] = trail[n]
 
@@ -305,26 +291,30 @@
             else:
                 acc[...] += step
 
-    def relay(h, k):
-        z_relay(h, k)
-        z_rest(h, k, -1)
-        z_rest(h, k, 1)
-
-    relay(h0, 0)
     arrive(arrived.at[:, SHARE:ROWS], body_sem)
     for half in range(2):
-        s1[c, half, y] = with_parcels(half * HALF, (half + 1) * HALF)
-    s_start(s1, 1)
-    relay(h1, 1)
-    s_cross(s0, 0)
+        extra = with_parcels(half * HALF, (half + 1) * HALF)
+        for e in range(EXTRA):
+            s1[c, half, lanes(e), :] = extra[:, lanes(e)].T
     s_cross(s1, 1)
+    for place_on_line in range(5, ZL):
+        token(place_on_line)
+    for h, k in heads:
+        z_relay(h, k)
+        for n in (1, 2):
+            z_rest(h, k, origins[n])
+            y_start(h, k, n)
     for s, k in ((s0, 0), (s1, 1)):
-        arrive(s.at[1 - c], sc_sems.at[k])
+        arrive(s.at[1 - c], s_sems.at[k])
+    for n in range(3):
+        y_rest(n)
     product(0)
     for h, k in heads:
         z_rest(h, k, 2)
+        y_start(h, k, 3)
+    x_reduce(0)
+    y_rest(3)
     product(1)
-    x_reduce(0)
     x_reduce(1)
     z_reduce(0)
     z_reduce(1)
@@ -332,11 +322,11 @@
         copy.wait()
     gather(0)
     gather(1)
-    spread(0)
     finish(0)
-    place(0)
     finish(1)
     finished = acc[...].astype(BF16)
+    spread(0)
+    place(0)
     spread(1)
     place(1)
     loads[5].wait()
@@ -352,7 +342,6 @@
 
 def body(border, col_index, barrier, counts, inverse, slab):
     dma = pltpu.SemaphoreType.DMA
-    wide = HELD // X
     return pl.pallas_call(
         kernel,
         out_shape=jax.ShapeDtypeStruct(slab.shape, slab.dtype),
@@ -366,23 +355,23 @@
             pltpu.VMEM(slab.shape, slab.dtype),
             pltpu.VMEM((SURPLUS, ROWS, W1), BF16),
             pltpu.VMEM((SURPLUS, ROWS, W1), BF16),
-            pltpu.VMEM((CORES, 2, Y, HALF, W0), BF16),
-            pltpu.VMEM((CORES, 2, Y, HALF, W1), BF16),
-            pltpu.VMEM((ZH, SHARE, W0), BF16),
-            pltpu.VMEM((ZH, SHARE, W1), BF16),
-            pltpu.VMEM((ZH, X, SHARE, wide), BF16),
-            pltpu.VMEM((ZH, X, SHARE, wide), BF16),
+            pltpu.VMEM((CORES, 2, W0, HALF), BF16),
+            pltpu.VMEM((CORES, 2, W1, HALF), BF16),
+            pltpu.VMEM((ZH, Y, SHARE, W0), BF16),
+            pltpu.VMEM((ZH, Y, SHARE, W1), BF16),
+            pltpu.VMEM((ZH, X, Y, SHARE, HALF), BF16),
+            pltpu.VMEM((ZH, X, Y, SHARE, HALF), BF16),
             pltpu.VMEM((ZH, Y, SHARE, HALF), BF16),
             pltpu.VMEM((ZH, ZL, SHARE, HALF), BF16),
             pltpu.VMEM((ZH, SHARE, HALF), BF16),
             pltpu.VMEM((ZH, Y, SHARE, HALF), BF16),
-            pltpu.VMEM((ZH, Y * CORES, SHARE, ROWS), BF16),
+            pltpu.VMEM((ZH, Y, CORES, SHARE, ROWS), BF16),
             pltpu.VMEM((ZH, Y, CORES, SHARE, HALF), BF16),
             pltpu.VMEM((Y, ZH, CORES, SHARE, HALF), BF16),
             pltpu.VMEM((ZH, Y, CORES * SHARE, PANEL), BF16),
             pltpu.VMEM((ROWS, PANEL), F32),
-            dma((128,)), dma((6,)), dma((ZH,)), dma, dma, dma((2,)), dma((2,)), dma((2, 2, 3)),
-            dma((2,)), dma((2,)), dma((2,)), dma((2,)), dma((2,)), dma((2,)), dma((2,)),
+            dma((128,)), dma((6,)), dma((ZH,)), dma, dma, dma((2,)), dma((2, 4)), dma((2, 2, 3)),
+            dma((2,)), dma((2,)), dma((2,)), dma((2,)), dma((2,)), dma((2,)),
             pltpu.SemaphoreType.REGULAR, pltpu.SemaphoreType.REGULAR,
         ],
         compiler_params=pltpu.CompilerParams(

time: 92 us -> 86.2 us (0.937)
  the two profiles are of different devices: /device:TPU:1 before, /device:TPU:9 now
where the time goes in v5:
time: 86.2 us; the launch traced here: 86 us
  Pallas kernels  84.4 us (98%)
  local copies, waits for them, and re-layouts  1.57 us (2%)
    pallas_call x1, Pallas kernels, body(): pl.pallas_call(kernel, out_shape=jax.ShapeDtypeStruct(slab.shape, slab.dt...  84.4 us

profile of v5, /device:TPU:9, one launch (start us, length us, event | category | flops | bytes accessed | tf_op | source)
XLA Modules:
  0.0 86.0 jit_solution(14286416462384842542)
XLA Ops:
  0.0 84.4 %panel_update.1 = f32[256,128]{1,0:T(8,128)} custom-call(s32[32]{0:T(128)} %counts_in.1, s32[16,128]{1,0:T(8,128)} %index_in.1, f32[32,128]{1,0:T(8,128)} %bitcast.3, bf16[16,256,128]{2,1,0:T(8,128)(2,1)} %border_in.1, bf16[4,4,64,1024]{3,2,1,0:T(8,128)(2,1)} %bitcast.2, f32[256,128]{1,0:T(8,128)} %slab_in.1), custom_call_target="tpu_custom_call" | custom-call | tf_op jit(solution)/shard_map/panel_update/pallas_call | solution.py:345
  84.4 1.6 %copy.8 = f32[256,128]{1,0:T(8,128)} copy(f32[256,128]{1,0:T(8,128)} %panel_update.1) | data formatting | bytes 262144

commit v6 on v5

--- a/solution.py
+++ b/solution.py
@@ -12,7 +12,7 @@
 ROWS, SHARE, PANEL, HALF = 256, 32, 1024, 128
 SEG = PANEL // ZH
 OWNER_OF = (3, 4, 2, 5)
-GROUPS = ((0, 3), (3, 4))
+GROUPS = ((0, 1), (1, 3), (3, 4))
 F32, BF16 = jnp.float32, jnp.bfloat16
 
 
@@ -204,7 +204,7 @@
     token(3)
     token(4)
 
-    group_of = {0: slice(*GROUPS[0]), 1: slice(*GROUPS[1])}
+    group_of = [slice(*group) for group in GROUPS]
 
     def product(g):
         first, last = GROUPS[g]
@@ -299,36 +299,47 @@
     s_cross(s1, 1)
     for place_on_line in range(5, ZL):
         token(place_on_line)
-    for h, k in heads:
+    def relay(h, k):
         z_relay(h, k)
         for n in (1, 2):
             z_rest(h, k, origins[n])
             y_start(h, k, n)
+
+    relay(h0, 0)
     for s, k in ((s0, 0), (s1, 1)):
         arrive(s.at[1 - c], s_sems.at[k])
-    for n in range(3):
-        y_rest(n)
+    y_rest(0)
     product(0)
+    relay(h1, 1)
+    x_reduce(0)
+    y_rest(1)
+    y_rest(2)
+    product(1)
     for h, k in heads:
         z_rest(h, k, 2)
         y_start(h, k, 3)
-    x_reduce(0)
+    z_reduce(0)
     y_rest(3)
-    product(1)
+    product(2)
     x_reduce(1)
-    z_reduce(0)
+    x_reduce(2)
+    gather(0)
     z_reduce(1)
+    z_reduce(2)
     for copy in inv_copies:
         copy.wait()
-    gather(0)
+    finish(0)
     gather(1)
-    finish(0)
+    gather(2)
+    spread(0)
     finish(1)
+    finish(2)
     finished = acc[...].astype(BF16)
-    spread(0)
     place(0)
-    spread(1)
-    place(1)
+    for g in (1, 2):
+        spread(g)
+    for g in (1, 2):
+        place(g)
     loads[5].wait()
     update = jnp.dot(finished, natural[...].reshape(PANEL, HALF), preferred_element_type=F32)
     out[...] = slab[...] - update
@@ -371,7 +382,7 @@
             pltpu.VMEM((ZH, Y, CORES * SHARE, PANEL), BF16),
             pltpu.VMEM((ROWS, PANEL), F32),
             dma((128,)), dma((6,)), dma((ZH,)), dma, dma, dma((2,)), dma((2, 4)), dma((2, 2, 3)),
-            dma((2,)), dma((2,)), dma((2,)), dma((2,)), dma((2,)), dma((2,)),
+            dma((3,)), dma((3,)), dma((3,)), dma((3,)), dma((3,)), dma((3,)),
             pltpu.SemaphoreType.REGULAR, pltpu.SemaphoreType.REGULAR,
         ],
         compiler_params=pltpu.CompilerParams(

time: 86.2 us -> 82.3 us (0.955)
  Pallas kernels: 84.4 us -> 80.5 us
    pallas_call x1, Pallas kernels: 84.4 us -> 80.5 us  [body(): pl.pallas_call(kernel, out_shape=jax.ShapeDtypeStruct(slab.shape, slab.dt...]
where the time goes in v6:
time: 82.3 us; the launch traced here: 82.1 us
  Pallas kernels  80.5 us (98%)
  local copies, waits for them, and re-layouts  1.57 us (2%)
    pallas_call x1, Pallas kernels, body(): pl.pallas_call(kernel, out_shape=jax.ShapeDtypeStruct(slab.shape, slab.dt...  80.5 us

profile of v6, /device:TPU:9, one launch (start us, length us, event | category | flops | bytes accessed | tf_op | source)
XLA Modules:
  0.0 82.1 jit_solution(11747024606252405722)
XLA Ops:
  0.0 80.5 %panel_update.1 = f32[256,128]{1,0:T(8,128)} custom-call(s32[32]{0:T(128)} %counts_in.1, s32[16,128]{1,0:T(8,128)} %index_in.1, f32[32,128]{1,0:T(8,128)} %bitcast.3, bf16[16,256,128]{2,1,0:T(8,128)(2,1)} %border_in.1, bf16[4,4,64,1024]{3,2,1,0:T(8,128)(2,1)} %bitcast.2, f32[256,128]{1,0:T(8,128)} %slab_in.1), custom_call_target="tpu_custom_call" | custom-call | tf_op jit(solution)/shard_map/panel_update/pallas_call | solution.py:356
  80.5 1.6 %copy.8 = f32[256,128]{1,0:T(8,128)} copy(f32[256,128]{1,0:T(8,128)} %panel_update.1) | data formatting | bytes 262144
